TPU v7x, 32 devices: a whole 2x2x4 slice. The times are simulated.
32 devices in a mesh: sensor: 4 (over y, core), space: 8 (over z, x).
Axes of the slice: x: 2, y: 2, z: 4, core: 2. Of those that a mesh axis runs over, the one named last changes fastest.
Arguments:
- jacobian: float32 [512, 16384], P('space', 'sensor'), as said below
- residual: float32 [16384], P('sensor'), may hold values from -6 to 6
- damping: float32 [1], replicated, may hold values from 0.3 to 3
Outputs:
- update: float32 [512], replicated
Inputs may be any that keep to these rules, and one draw needn't show every extreme that they name: `jacobian`: every column block of the Jacobian has full rank over any 512 observations, which number at least the parameters; the entries are real-valued with row and column scales that vary.
All inputs are finite; a program needn't handle non-finite values.
Results may differ from a plain program's by a relative error of at most 0.00011.
Values sent between devices are 32-bit elements; how exact they have to be, the bound alone decides.
No kernel may reach another device: no remote copies, remote signals or barrier semaphores. Data moves between devices by JAX's collectives and lax.ppermute only.
A program may use at most 64 MiB of HBM per device.

v0:
```python
import jax
import jax.numpy as jnp
from jax import lax
from jax.sharding import PartitionSpec as P


def per_device(jacobian, residual, damping):
    high = lax.Precision.HIGHEST
    columns = jacobian.shape[0]
    groups = lax.axis_size("space")
    params_all = columns * groups
    part_grad = jnp.dot(jacobian, residual, precision=high)
    grad_local = lax.dynamic_update_slice(
        jnp.zeros((params_all,), jnp.float32), part_grad, (lax.axis_index("space") * columns,)
    )
    panel_t = lax.all_to_all(jacobian, "space", split_axis=1, concat_axis=0, tiled=True)
    gram_local = lax.dot_general(panel_t, panel_t, (((1,), (1,)), ((), ())), precision=high)
    gram_group, grad_group = lax.psum((gram_local, grad_local), "space")
    gram_all, grad_all = lax.psum((gram_group, grad_group), "sensor")
    damped = gram_all + damping[0] * jnp.diag(jnp.diag(gram_all))
    factor = jnp.linalg.cholesky(damped)
    return -jax.scipy.linalg.cho_solve((factor, True), grad_all)


def solution(mesh):
    placed = (P("space", "sensor"), P("sensor"), P())
    return jax.shard_map(per_device, mesh=mesh, in_specs=placed, out_specs=P(), check_vma=False)
```

profile of v0, /device:TPU:0, one launch (start us, length us, event | category | flops | bytes accessed | tf_op | source)
XLA Modules:
  0.0 311.7 jit_solution(12249171158985935714)
XLA Ops:
  6.5 1.3 copy.52
  7.9 32.8 %all_to_all.19 = f32[64,8,512]{2,0,1:T(8,128)S(1)} all-to-all(f32[64,8,512]{2,0,1:T(8,128)S(1)} %bitcast.158), channel_id=1, replica_groups=mesh['sensor'=4,'space'=8] {'space'}, dimensions={1} | all-to-all | bytes 2097152 | tf_op jit(solution)/shard_map/all_to_all | solution.py:16
  40.7 2.9 fusion.57
  43.7 77.3 %all-reduce.4.cloned.1.call-done = f32[512,512]{0,1:T(8,128)} async-done(((f32[512,512]{0,1:T(8,128)}), f32[512,512]{0,1:T(8,128)}) %all-reduce.4.cloned.1.call-update) | async-done | bytes 1048592 | tf_op jit(solution)/shard_map/psum | solution.py:18
  121.7 0.9 convolution_bitcast_fusion
  122.6 0.2 dynamic_update_slice.3
  122.8 20.0 %psum.30 = f32[512]{0:T(512)S(1)} all-reduce(f32[512]{0:T(512)S(1)} %dynamic_update_slice.3), channel_id=1, replica_groups=mesh['sensor'=4,'space'=8] {'space'}, use_global_device_ids=true, to_apply=%region_10.11 | all-reduce | flops 512 | bytes 4096 | tf_op jit(solution)/shard_map/psum | solution.py:18
  142.8 5.6 %psum.31 = f32[512]{0:T(512)S(1)} all-reduce(f32[512]{0:T(512)S(1)} %psum.30), channel_id=1, replica_groups=mesh['sensor'=4,'space'=8] {'sensor'}, use_global_device_ids=true, to_apply=%region_11.12 | all-reduce | flops 512 | bytes 4096 | tf_op jit(solution)/shard_map/psum | solution.py:19
  148.5 10.8 %all-reduce.6.cloned.1.call-done = f32[512,512]{0,1:T(8,128)} async-done(((f32[512,512]{0,1:T(8,128)}), f32[512,512]{0,1:T(8,128)}) %all-reduce.6.cloned.1.call-update) | async-done | bytes 1048592 | tf_op jit(solution)/shard_map/psum | solution.py:19
  159.3 8.7 %gather_fusion = f32[512]{0:T(512)S(1)} fusion(f32[512,512]{0,1:T(8,128)} %all-reduce.6.cloned.1.call-done, s32[512]{0:T(512)S(1)} %bitcast.155), kind=kCustom, calls=%fused_computation | custom fusion | bytes 8192 | tf_op jit(solution)/shard_map/jit(_diag)/jit(diagonal)/cond/branch_0_fun/gather | solution.py:20
  168.1 0.3 copy.37
  168.4 0.2 fusion.12
  168.7 11.7 %cholesky.103 = f32[128,128]{1,0:T(8,128)S(1)} custom-call(f32[128,128]{1,0:T(8,128)S(1)} %cholesky.263), custom_call_target="Cholesky" | custom-call | tf_op jit(solution)/shard_map/jit(cholesky)/cholesky | solution.py:21
  180.6 9.8 %custom-call.34 = f32[1,128,128]{1,2,0:T(8,128)S(1)} custom-call(f32[1,128,128]{2,1,0:T(8,128)S(1)} %get-tuple-element.44), custom_call_target="InvertDiagBlocksLowerTriangular" | custom-call | tf_op jit(solution)/shard_map/jit(cholesky)/cholesky | solution.py:21
  190.4 0.3 fusion.17
  190.8 0.3 convolution_subtract_fusion
  191.2 11.7 %cholesky.215 = f32[128,128]{1,0:T(8,128)S(1)} custom-call(f32[128,128]{1,0:T(8,128)S(1)} %cholesky.267), custom_call_target="Cholesky" | custom-call | tf_op jit(solution)/shard_map/jit(cholesky)/cholesky | solution.py:21
  203.2 10.0 %custom-call.35 = f32[1,128,128]{1,2,0:T(8,128)S(1)} custom-call(f32[1,128,128]{2,1,0:T(8,128)S(1)} %get-tuple-element.42), custom_call_target="InvertDiagBlocksLowerTriangular" | custom-call | tf_op jit(solution)/shard_map/jit(cholesky)/cholesky | solution.py:21
  213.2 0.3 convolution_dynamic-update-slice_fusion
  213.5 0.6 convolution_subtract_fusion.1
  214.1 11.7 %cholesky.236 = f32[128,128]{1,0:T(8,128)S(1)} custom-call(f32[128,128]{1,0:T(8,128)S(1)} %cholesky.272), custom_call_target="Cholesky" | custom-call | tf_op jit(solution)/shard_map/jit(cholesky)/cholesky | solution.py:21
  226.0 9.8 %custom-call.36 = f32[1,128,128]{1,2,0:T(8,128)S(1)} custom-call(f32[1,128,128]{2,1,0:T(8,128)S(1)} %get-tuple-element.40), custom_call_target="InvertDiagBlocksLowerTriangular" | custom-call | tf_op jit(solution)/shard_map/jit(cholesky)/cholesky | solution.py:21
  235.8 0.3 convolution_dynamic-update-slice_fusion.1
  236.1 0.5 convolution_subtract_fusion.2
  236.6 11.9 %cholesky.253 = f32[128,128]{1,0:T(8,128)S(1)} custom-call(f32[128,128]{1,0:T(8,128)S(1)} %convolution_subtract_fusion.2), custom_call_target="Cholesky" | custom-call | tf_op jit(solution)/shard_map/jit(cholesky)/cholesky | solution.py:21
  248.7 0.7 compare_reduce_fusion.1
  249.4 0.6 compare_reduce_fusion
  250.1 0.7 compare_reduce_fusion.2
  253.4 8.6 %while.1 = (s32[]{:T(128)}, f32[512,512]{0,1:T(8,128)S(1)}, s32[4,2]{0,1:T(2,128)S(1)}, f32[4,128,128]{2,1,0:T(8,128)S(1)}, s32[]{:T(128)}) while((s32[]{:T(128)}, f32[512,512]{0,1:T(8,128)S(1)}, s32[4,2]{0,1:T(2,128)S(1)}, f32[4,128,128]{2,1,0:T(8,128)S(1)}, s32[]{:T(128)}) %tuple.27), condition=%wide.while_cond, body=%wide.while_body.sunk | while | flops 2 | bytes 393329 | solution.py:22
  253.5 0.6 fusion.72
  254.1 1.3 dynamic-slice.7
  255.7 0.6 fusion.72
  256.3 1.3 dynamic-slice.7
  257.8 0.6 fusion.72
  258.4 1.3 dynamic-slice.7
  260.0 0.6 fusion.72
  260.6 1.3 dynamic-slice.7
  262.0 39.3 %custom-call.37 = f32[4,128,128]{1,2,0:T(8,128)S(1)} custom-call(f32[4,128,128]{2,1,0:T(8,128)S(1)} %get-tuple-element.12), custom_call_target="InvertDiagBlocksLowerTriangular" | custom-call | tf_op jit(solution)/shard_map/jit(_cho_solve)/triangular_solve | solution.py:22
  301.9 0.2 fusion.6
  302.2 0.2 fusion.11
  302.6 0.2 convolution_bitcast_fusion.6
  302.8 0.2 fusion.2
  303.1 0.2 convolution_bitcast_fusion.4
  303.3 0.2 fusion.7
  303.5 0.2 convolution_bitcast_fusion.2
  303.7 0.3 fusion.9
  304.0 0.2 convolution_bitcast_fusion.1
  304.3 0.6 maximum_negate_fusion
  (51 shorter events, 2.7 us)
Async XLA Ops:
  6.5 115.1 %copy-start = (f32[4096]{0:T(1024)S(1)}, f32[4096]{0:T(1024)}, u32[]{:S(2)}) copy-start(f32[4096]{0:T(1024)} %param.4) | copy-start | bytes 49156
  6.5 114.4 %all-reduce.4.cloned.1.call-start = ((), (), s32[]{:S(2)}) async-start(), calls=%async_computation.1 | async-start | bytes 2097152 | tf_op jit(solution)/shard_map/psum | solution.py:18
  43.6 78.1 %copy-start.2 = (f32[64,4096]{1,0:T(8,128)S(1)}, f32[64,4096]{1,0:T(8,128)}, u32[]{:S(2)}) copy-start(f32[64,4096]{1,0:T(8,128)} %param.3) | copy-start | bytes 3145732
  43.6 115.6 %all-reduce.6.cloned.1.call-start = ((), (), s32[]{:S(2)}) async-start(), calls=%async_computation.2 | async-start | bytes 2097152 | tf_op jit(solution)/shard_map/psum | solution.py:19
  159.3 8.7 %copy-start.1 = (f32[512,512]{0,1:T(8,128)S(1)}, f32[512,512]{0,1:T(8,128)}, u32[]{:S(2)}) copy-start(f32[512,512]{0,1:T(8,128)} %all-reduce.6.cloned.1.call-done) | copy-start | bytes 3145732
Sparse Core Ops, SparseCore 0:
  43.8 77.1 all-reduce.3
  123.3 35.8 all-reduce.5
where the time goes:
time: 312 us
  other arithmetic  119 us (38%)
  waiting for transfers between devices  88.1 us (28%)
  blocking collectives  58.5 us (19%)
  local copies, waits for them, and re-layouts  19.7 us (6%)
  between operations  16.9 us (5%)
  matrix products  9.06 us (3%)
    another operation x14, other arithmetic, per_device(): factor = jnp.linalg.cholesky(damped)  78.9 us
    psum x1, waiting for transfers between devices, per_device(): gram_group, grad_group = lax.psum((gram_local, grad_local), 'space')  77.3 us
    another operation x3, other arithmetic, per_device(): return -jax.scipy.linalg.cho_solve((factor, True), grad_all)  39.4 us
    all_to_all x1, blocking collectives, per_device(): lax.all_to_all(jacobian, 'space', split_axis=1, concat_axis=0, tiled=True)  32.8 us
    psum x1, blocking collectives, per_device(): gram_group, grad_group = lax.psum((gram_local, grad_local), 'space')  20 us
    psum x1, waiting for transfers between devices, per_device(): gram_all, grad_all = lax.psum((gram_group, grad_group), 'sensor')  10.8 us
    gather x1, local copies, waits for them, and re-layouts, per_device(): damped = gram_all + damping[0] * jnp.diag(jnp.diag(gram_all))  8.67 us
    another operation x20, local copies, waits for them, and re-layouts  8.46 us
  transfers between devices with their start and end apart: 2, of which 2 were waited for; matrix products, arithmetic and copies ran while one was open for 0% of the time, Pallas kernels for 0%

commit v1 on v0

--- a/solution.py
+++ b/solution.py
@@ -2,6 +2,29 @@
 import jax.numpy as jnp
 from jax import lax
 from jax.sharding import PartitionSpec as P
+
+
+def in_blocks(x, dim, size):
+    shape = x.shape
+    blocks = x.reshape(*shape[:dim], size, shape[dim] // size, *shape[dim + 1 :])
+    return jnp.moveaxis(blocks, dim, 0)
+
+
+def joined_along(blocks, dim):
+    blocks = jnp.moveaxis(blocks, 0, dim)
+    shape = blocks.shape
+    return blocks.reshape(*shape[:dim], shape[dim] * shape[dim + 1], *shape[dim + 2 :])
+
+
+def sent_to_each(value, axis, split_dim, concat_dim):
+    devices, mine = (lax.axis_size(axis), lax.axis_index(axis))
+    pieces = in_blocks(value, split_dim, devices)
+    done = [pieces[mine]]
+    for lap in range(1, devices):
+        sent = pieces[(mine + lap) % devices]
+        done.append(lax.ppermute(sent, axis, [(i, (i + lap) % devices) for i in range(devices)]))
+    pieces = jnp.stack(done)[(mine - jnp.arange(devices)) % devices]
+    return joined_along(pieces, concat_dim)
 
 
 def per_device(jacobian, residual, damping):
@@ -13,7 +36,7 @@
     grad_local = lax.dynamic_update_slice(
         jnp.zeros((params_all,), jnp.float32), part_grad, (lax.axis_index("space") * columns,)
     )
-    panel_t = lax.all_to_all(jacobian, "space", split_axis=1, concat_axis=0, tiled=True)
+    panel_t = sent_to_each(jacobian, "space", 1, 0)
     gram_local = lax.dot_general(panel_t, panel_t, (((1,), (1,)), ((), ())), precision=high)
     gram_group, grad_group = lax.psum((gram_local, grad_local), "space")
     gram_all, grad_all = lax.psum((gram_group, grad_group), "sensor")

time: 312 us -> 312 us (level)
  blocking collectives: 58.5 us -> 25.7 us
  waiting for transfers between devices: 88.1 us -> 103 us
  starting transfers between devices: 0.04 us -> 14.3 us
    all_to_all x1 -> x0, blocking collectives: 32.8 us -> none  [per_device(): lax.all_to_all(jacobian, 'space', split_axis=1, concat_axis=0, tiled=True)]
    ppermute x0 -> x7, starting transfers between devices: none -> 14.3 us  [sent_to_each(): lax.ppermute(sent, axis, [(i, (i + lap) % devices) for i in range(devices)])]
    psum x1, waiting for transfers between devices: 77.3 us -> 85.7 us  [per_device(): gram_group, grad_group = lax.psum((gram_local, grad_local), 'space')]
    ppermute x0 -> x7, waiting for transfers between devices: none -> 6.86 us  [sent_to_each(): lax.ppermute(sent, axis, [(i, (i + lap) % devices) for i in range(devices)])]
    another operation x20 -> x22, local copies, waits for them, and re-layouts: 8.46 us -> 9.53 us
  transfers between devices with their start and end apart: 2 -> 9, of which waited for: 2 -> 4; matrix products, arithmetic and copies ran while one was open for 0% -> 0% of each run, Pallas kernels for 0% -> 0%
where the time goes in v1:
time: 312 us; the launch traced here: 311 us
  other arithmetic  119 us (38%)
  waiting for transfers between devices  103 us (33%)
  blocking collectives  25.7 us (8%)
  local copies, waits for them, and re-layouts  22 us (7%)
  between operations  17 us (5%)
  starting transfers between devices  14.3 us (5%)
  matrix products  9.05 us (3%)
    psum x1, waiting for transfers between devices, per_device(): gram_group, grad_group = lax.psum((gram_local, grad_local), 'space')  85.7 us
    another operation x14, other arithmetic, per_device(): factor = jnp.linalg.cholesky(damped)  78.9 us
    another operation x3, other arithmetic, per_device(): return -jax.scipy.linalg.cho_solve((factor, True), grad_all)  39.4 us
    psum x1, blocking collectives, per_device(): gram_group, grad_group = lax.psum((gram_local, grad_local), 'space')  20 us
    ppermute x7, starting transfers between devices, sent_to_each(): lax.ppermute(sent, axis, [(i, (i + lap) % devices) for i in range(devices)])  14.3 us
    psum x1, waiting for transfers between devices, per_device(): gram_all, grad_all = lax.psum((gram_group, grad_group), 'sensor')  10.8 us
    another operation x21, local copies, waits for them, and re-layouts  9.52 us
    gather x1, local copies, waits for them, and re-layouts, per_device(): damped = gram_all + damping[0] * jnp.diag(jnp.diag(gram_all))  8.67 us
  transfers between devices with their start and end apart: 9, of which 4 were waited for; matrix products, arithmetic and copies ran while one was open for 0% of the time, Pallas kernels for 0%

profile of v1, /device:TPU:0, one launch (start us, length us, event | category | flops | bytes accessed | tf_op | source)
XLA Modules:
  0.0 311.1 jit_solution(12578675553524134155)
XLA Ops:
  6.5 1.8 copy.36
  8.4 1.1 constant_dynamic-slice_fusion.1
  9.5 3.0 collective-permute-start
  12.5 1.6 collective-permute-start.1
  14.2 2.6 collective-permute-start.2
  16.8 1.3 collective-permute-start.3
  18.1 2.7 collective-permute-start.4
  20.9 1.4 collective-permute-start.5
  22.3 1.7 collective-permute-start.6
  24.0 6.4 %collective-permute-done.2 = f32[64,512]{1,0:T(8,128)S(1)} collective-permute-done((f32[64,512]{1,0:T(8,128)S(1)}, f32[64,512]{1,0:T(8,128)S(1)}, u32[]{:S(2)}, u32[]{:S(2)}) %collective-permute-start.2) | collective-permute-done | bytes 131104 | tf_op jit(solution)/shard_map/ppermute | solution.py:25
  30.4 0.4 collective-permute-done.3
  30.9 0.6 gather_fusion
  31.6 2.9 fusion.59
  34.5 85.7 %all-reduce.4.cloned.1.call-done = f32[512,512]{0,1:T(8,128)} async-done(((f32[512,512]{0,1:T(8,128)}), f32[512,512]{0,1:T(8,128)}) %all-reduce.4.cloned.1.call-update) | async-done | bytes 1048592 | tf_op jit(solution)/shard_map/psum | solution.py:41
  121.0 0.9 convolution_bitcast_fusion
  122.1 20.0 %psum.30 = f32[512]{0:T(512)S(1)} all-reduce(f32[512]{0:T(512)S(1)} %dynamic_update_slice.3), channel_id=1, replica_groups=mesh['sensor'=4,'space'=8] {'space'}, use_global_device_ids=true, to_apply=%region_10.11 | all-reduce | flops 512 | bytes 4096 | tf_op jit(solution)/shard_map/psum | solution.py:41
  142.1 5.6 %psum.31 = f32[512]{0:T(512)S(1)} all-reduce(f32[512]{0:T(512)S(1)} %psum.30), channel_id=1, replica_groups=mesh['sensor'=4,'space'=8] {'sensor'}, use_global_device_ids=true, to_apply=%region_11.12 | all-reduce | flops 512 | bytes 4096 | tf_op jit(solution)/shard_map/psum | solution.py:42
  147.8 10.8 %all-reduce.6.cloned.1.call-done = f32[512,512]{0,1:T(8,128)} async-done(((f32[512,512]{0,1:T(8,128)}), f32[512,512]{0,1:T(8,128)}) %all-reduce.6.cloned.1.call-update) | async-done | bytes 1048592 | tf_op jit(solution)/shard_map/psum | solution.py:42
  158.6 8.7 %gather_fusion.1 = f32[512]{0:T(512)S(1)} fusion(f32[512,512]{0,1:T(8,128)} %all-reduce.6.cloned.1.call-done, s32[512]{0:T(512)S(1)} %bitcast.190), kind=kCustom, calls=%fused_computation.1 | custom fusion | bytes 8192 | tf_op jit(solution)/shard_map/jit(_diag)/jit(diagonal)/cond/branch_0_fun/gather | solution.py:43
  167.4 0.3 copy.15
  168.0 11.7 %cholesky.103 = f32[128,128]{1,0:T(8,128)S(1)} custom-call(f32[128,128]{1,0:T(8,128)S(1)} %cholesky.263), custom_call_target="Cholesky" | custom-call | tf_op jit(solution)/shard_map/jit(cholesky)/cholesky | solution.py:44
  179.9 9.8 %custom-call.34 = f32[1,128,128]{1,2,0:T(8,128)S(1)} custom-call(f32[1,128,128]{2,1,0:T(8,128)S(1)} %get-tuple-element.44), custom_call_target="InvertDiagBlocksLowerTriangular" | custom-call | tf_op jit(solution)/shard_map/jit(cholesky)/cholesky | solution.py:44
  189.7 0.3 fusion.17
  190.1 0.3 convolution_subtract_fusion
  190.5 11.7 %cholesky.215 = f32[128,128]{1,0:T(8,128)S(1)} custom-call(f32[128,128]{1,0:T(8,128)S(1)} %cholesky.267), custom_call_target="Cholesky" | custom-call | tf_op jit(solution)/shard_map/jit(cholesky)/cholesky | solution.py:44
  202.5 10.0 %custom-call.35 = f32[1,128,128]{1,2,0:T(8,128)S(1)} custom-call(f32[1,128,128]{2,1,0:T(8,128)S(1)} %get-tuple-element.42), custom_call_target="InvertDiagBlocksLowerTriangular" | custom-call | tf_op jit(solution)/shard_map/jit(cholesky)/cholesky | solution.py:44
  212.5 0.3 convolution_dynamic-update-slice_fusion
  212.9 0.6 convolution_subtract_fusion.1
  213.5 11.7 %cholesky.236 = f32[128,128]{1,0:T(8,128)S(1)} custom-call(f32[128,128]{1,0:T(8,128)S(1)} %cholesky.272), custom_call_target="Cholesky" | custom-call | tf_op jit(solution)/shard_map/jit(cholesky)/cholesky | solution.py:44
  225.3 9.8 %custom-call.36 = f32[1,128,128]{1,2,0:T(8,128)S(1)} custom-call(f32[1,128,128]{2,1,0:T(8,128)S(1)} %get-tuple-element.40), custom_call_target="InvertDiagBlocksLowerTriangular" | custom-call | tf_op jit(solution)/shard_map/jit(cholesky)/cholesky | solution.py:44
  235.1 0.3 convolution_dynamic-update-slice_fusion.1
  235.4 0.5 convolution_subtract_fusion.2
  235.9 11.9 %cholesky.253 = f32[128,128]{1,0:T(8,128)S(1)} custom-call(f32[128,128]{1,0:T(8,128)S(1)} %convolution_subtract_fusion.2), custom_call_target="Cholesky" | custom-call | tf_op jit(solution)/shard_map/jit(cholesky)/cholesky | solution.py:44
  248.0 0.7 compare_reduce_fusion.1
  248.7 0.6 compare_reduce_fusion
  249.4 0.7 compare_reduce_fusion.2
  252.7 8.6 %while.1 = (s32[]{:T(128)}, f32[512,512]{0,1:T(8,128)S(1)}, s32[4,2]{0,1:T(2,128)S(1)}, f32[4,128,128]{2,1,0:T(8,128)S(1)}, s32[]{:T(128)}) while((s32[]{:T(128)}, f32[512,512]{0,1:T(8,128)S(1)}, s32[4,2]{0,1:T(2,128)S(1)}, f32[4,128,128]{2,1,0:T(8,128)S(1)}, s32[]{:T(128)}) %tuple.32), condition=%wide.while_cond, body=%wide.while_body.sunk | while | flops 2 | bytes 393329 | solution.py:45
  252.8 0.6 fusion.74
  253.4 1.3 dynamic-slice.47
  255.0 0.6 fusion.74
  255.6 1.3 dynamic-slice.47
  257.1 0.6 fusion.74
  257.7 1.3 dynamic-slice.47
  259.3 0.6 fusion.74
  259.9 1.3 dynamic-slice.47
  261.3 39.3 %custom-call.37 = f32[4,128,128]{1,2,0:T(8,128)S(1)} custom-call(f32[4,128,128]{2,1,0:T(8,128)S(1)} %get-tuple-element.12), custom_call_target="InvertDiagBlocksLowerTriangular" | custom-call | tf_op jit(solution)/shard_map/jit(_cho_solve)/triangular_solve | solution.py:45
  303.0 0.3 fusion.9
  303.6 0.6 maximum_negate_fusion
  (83 shorter events, 5.1 us)
Async XLA Ops:
  6.5 114.4 %copy-start = (f32[4096]{0:T(1024)S(1)}, f32[4096]{0:T(1024)}, u32[]{:S(2)}) copy-start(f32[4096]{0:T(1024)} %param.4) | copy-start | bytes 49156
  6.5 113.8 %all-reduce.4.cloned.1.call-start = ((), (), s32[]{:S(2)}) async-start(), calls=%async_computation | async-start | bytes 2097152 | tf_op jit(solution)/shard_map/psum | solution.py:41
  9.5 11.4 %collective-permute-start = (f32[64,512]{1,0:T(8,128)S(1)}, f32[64,512]{1,0:T(8,128)S(1)}, u32[]{:S(2)}, u32[]{:S(2)}) collective-permute-start(f32[64,512]{1,0:T(8,128)S(1)} %bitcast.200), channel_id=1, source_target_pairs={{0,1},{1,2},{2,3},{3,4},{4,5},{5,6},{6,7},{7,0},{8,9},{9,10},{10,1... | collective-permute-start | bytes 393224 | tf_op jit(solution)/shard_map/ppermute | solution.py:25
  12.5 9.8 %collective-permute-start.1 = (f32[64,512]{1,0:T(8,128)S(1)}, f32[64,512]{1,0:T(8,128)S(1)}, u32[]{:S(2)}, u32[]{:S(2)}) collective-permute-start(f32[64,512]{1,0:T(8,128)S(1)} %bitcast.199), channel_id=1, source_target_pairs={{0,2},{1,3},{2,4},{3,5},{4,6},{5,7},{6,0},{7,1},{8,10},{9,11},{10,... | collective-permute-start | bytes 393224 | tf_op jit(solution)/shard_map/ppermute | solution.py:25
  14.2 16.2 %collective-permute-start.2 = (f32[64,512]{1,0:T(8,128)S(1)}, f32[64,512]{1,0:T(8,128)S(1)}, u32[]{:S(2)}, u32[]{:S(2)}) collective-permute-start(f32[64,512]{1,0:T(8,128)S(1)} %bitcast.197), channel_id=1, source_target_pairs={{0,3},{1,4},{2,5},{3,6},{4,7},{5,0},{6,1},{7,2},{8,11},{9,12},{10,... | collective-permute-start | bytes 393224 | tf_op jit(solution)/shard_map/ppermute | solution.py:25
  16.8 14.0 %collective-permute-start.3 = (f32[64,512]{1,0:T(8,128)S(1)}, f32[64,512]{1,0:T(8,128)S(1)}, u32[]{:S(2)}, u32[]{:S(2)}) collective-permute-start(f32[64,512]{1,0:T(8,128)S(1)} %bitcast.196), channel_id=1, source_target_pairs={{0,4},{1,5},{2,6},{3,7},{4,0},{5,1},{6,2},{7,3},{8,12},{9,13},{10,... | collective-permute-start | bytes 393224 | tf_op jit(solution)/shard_map/ppermute | solution.py:25
  18.1 12.7 %collective-permute-start.4 = (f32[64,512]{1,0:T(8,128)S(1)}, f32[64,512]{1,0:T(8,128)S(1)}, u32[]{:S(2)}, u32[]{:S(2)}) collective-permute-start(f32[64,512]{1,0:T(8,128)S(1)} %bitcast.195), channel_id=1, source_target_pairs={{0,5},{1,6},{2,7},{3,0},{4,1},{5,2},{6,3},{7,4},{8,13},{9,14},{10,... | collective-permute-start | bytes 393224 | tf_op jit(solution)/shard_map/ppermute | solution.py:25
  20.9 10.0 %collective-permute-start.5 = (f32[64,512]{1,0:T(8,128)S(1)}, f32[64,512]{1,0:T(8,128)S(1)}, u32[]{:S(2)}, u32[]{:S(2)}) collective-permute-start(f32[64,512]{1,0:T(8,128)S(1)} %bitcast.198), channel_id=1, source_target_pairs={{0,6},{1,7},{2,0},{3,1},{4,2},{5,3},{6,4},{7,5},{8,14},{9,15},{10,... | collective-permute-start | bytes 393224 | tf_op jit(solution)/shard_map/ppermute | solution.py:25
  22.3 8.6 %collective-permute-start.6 = (f32[64,512]{1,0:T(8,128)S(1)}, f32[64,512]{1,0:T(8,128)S(1)}, u32[]{:S(2)}, u32[]{:S(2)}) collective-permute-start(f32[64,512]{1,0:T(8,128)S(1)} %bitcast.194), channel_id=1, source_target_pairs={{0,7},{1,0},{2,1},{3,2},{4,3},{5,4},{6,5},{7,6},{8,15},{9,8},{10,9... | collective-permute-start | bytes 393224 | tf_op jit(solution)/shard_map/ppermute | solution.py:25
  34.5 86.5 %copy-start.2 = (f32[64,4096]{1,0:T(8,128)S(1)}, f32[64,4096]{1,0:T(8,128)}, u32[]{:S(2)}) copy-start(f32[64,4096]{1,0:T(8,128)} %param.3) | copy-start | bytes 3145732
  34.5 124.1 %all-reduce.6.cloned.1.call-start = ((), (), s32[]{:S(2)}) async-start(), calls=%async_computation.1 | async-start | bytes 2097152 | tf_op jit(solution)/shard_map/psum | solution.py:42
  158.6 8.7 %copy-start.1 = (f32[512,512]{0,1:T(8,128)S(1)}, f32[512,512]{0,1:T(8,128)}, u32[]{:S(2)}) copy-start(f32[512,512]{0,1:T(8,128)} %all-reduce.6.cloned.1.call-done) | copy-start | bytes 3145732
Sparse Core Ops, SparseCore 0:
  34.6 85.6 all-reduce.3
  122.7 35.8 all-reduce.5
